TPU v7x, 32 devices: a whole 2x2x4 slice. The times are simulated.
32 devices in a mesh: pole: 4 (over x, core), grid: 8 (over z, y).
Axes of the slice: x: 2, y: 2, z: 4, core: 2. Of those that a mesh axis runs over, the one named last changes fastest.
Arguments:
- anc_inv: bfloat16 [4, 1536, 1536], P('pole', 'grid'), may hold values from -6 to 6
- factor_cols: bfloat16 [4, 8, 2, 256, 256], P('pole', 'grid'), may hold values from -0.25 to 0.25
- diag_inv: bfloat16 [4, 8, 256, 256], P('pole', 'grid'), may hold values from -6 to 6
- intersection: bfloat16 [8, 256, 256], P('grid'), may hold values from -0.0234375 to 0.0234375
- pole_w: float32 [4], P('pole'), may hold values from 0.5 to 2
- pole_z: float32 [4], P('pole'), may hold values from -2 to -0.5
- ancestors: int32 [8, 2], P('grid'), may hold values from 0 to 5, as said below
- counts: int32 [8], P('grid'), may hold values from 1 to 2
- hpattern: int32 [8, 2], P('grid'), may hold values 0 or 1
- siesta_of: int32 [2048], P('grid'), may hold values from 0 to 2047, as said below
- supernode_of: int32 [2048], P('grid'), may hold values from 0 to 2047, as said below
Outputs:
- density: bfloat16 [2048, 768], P('grid', 'pole')
- energy: bfloat16 [2048, 768], P('grid', 'pole')
- electrons: float32 [], replicated
Inputs may be any that keep to these rules, and one draw needn't show every extreme that they name: `ancestors`: the 2 entries of a row are distinct. `siesta_of`: A permutation; supernode K's 256 orbitals go to each block-column owner (index // 256) at most 32 times, and exactly 32 times to some owner. `supernode_of`: the inverse permutation of siesta_of.
All inputs are finite; a program needn't handle non-finite values. No bound on the sum of `hpattern` on one device may be relied on, other than what follows from the above.
Results may differ from a plain program's by a relative error of at most 0.001.
Values may be sent and summed in bfloat16 or wider, within the bound.
No kernel may reach another device: no remote copies, remote signals or barrier semaphores. Data moves between devices by JAX's collectives and lax.ppermute only.
A program may use at most 64 MiB of HBM per device.

v0:
```python
import jax
import jax.numpy as jnp
from jax import lax
from jax.sharding import PartitionSpec as P


def body(
    anc_inv,
    factor_cols,
    diag_inv,
    intersection,
    pole_w,
    pole_z,
    ancestors,
    counts,
    hpattern,
    siesta_of,
    supernode_of,
):
    width = diag_inv.shape[-1]
    anc_count = anc_inv.shape[2] // width
    blk_count = ancestors.shape[1]
    select = (ancestors[0][:, None] == jnp.arange(anc_count)[None, :]).astype(jnp.bfloat16)
    live_mask = (jnp.arange(blk_count) < counts[0]).astype(jnp.bfloat16)
    lower_cols = (factor_cols[0, 0] * live_mask[:, None, None]).reshape(blk_count * width, width)
    gathered = lax.all_gather(anc_inv[0], "grid", axis=0, tiled=True)
    row_count = gathered.shape[0]
    picked = jnp.einsum(
        "rnw,mn->rmw",
        gathered.reshape(row_count, anc_count, width),
        select,
        preferred_element_type=jnp.float32,
    ).astype(jnp.bfloat16)
    product = jnp.dot(
        picked.reshape(row_count, blk_count * width), lower_cols, preferred_element_type=jnp.float32
    )
    blocks = product.reshape(anc_count, width, width)
    chosen = -jnp.sum(select.astype(jnp.float32)[:, :, None, None] * blocks[None], axis=1)
    diag_block = diag_inv[0, 0].astype(jnp.float32) - jnp.dot(
        lower_cols.astype(jnp.float32).T,
        chosen.reshape(blk_count * width, width),
        precision=lax.Precision.HIGHEST,
        preferred_element_type=jnp.float32,
    )
    masked = chosen * hpattern[0].astype(jnp.float32)[:, None, None]
    stacked = jnp.concatenate([diag_block[None], masked], axis=0)
    cols_rows = stacked.transpose(2, 0, 1).reshape(width, (blk_count + 1) * width)
    own_count = pole_w[0] * jnp.sum(diag_block * intersection[0].astype(jnp.float32))
    electrons = lax.psum(own_count, ("pole", "grid"))
    dens_term = pole_w[0] * cols_rows
    energy_term = pole_z[0] * cols_rows
    dens_part, energy_part = (
        lax.psum_scatter(dens_term, "pole", scatter_dimension=1, tiled=True),
        lax.psum_scatter(energy_term, "pole", scatter_dimension=1, tiled=True),
    )
    row_width = dens_part.shape[1]
    grid_count = lax.axis_size("grid")
    slot_cap = (width + grid_count - 1) // grid_count
    positions = jnp.arange(width)
    dest_owner = siesta_of // width
    same_dest = dest_owner[:, None] == dest_owner[None, :]
    earlier = positions[:, None] > positions[None, :]
    send_rank = jnp.sum((same_dest & earlier).astype(jnp.int32), axis=1)
    send_slot = dest_owner * slot_cap + send_rank
    placement = (jnp.arange(grid_count * slot_cap)[:, None] == send_slot[None, :]).astype(
        jnp.bfloat16
    )
    send_dens = (
        jnp.dot(placement, dens_part.astype(jnp.bfloat16), preferred_element_type=jnp.float32)
        .astype(jnp.bfloat16)
        .reshape(grid_count, slot_cap, row_width)
    )
    send_energy = (
        jnp.dot(placement, energy_part.astype(jnp.bfloat16), preferred_element_type=jnp.float32)
        .astype(jnp.bfloat16)
        .reshape(grid_count, slot_cap, row_width)
    )
    recv_dens, recv_energy = (
        lax.all_to_all(send_dens, "grid", split_axis=0, concat_axis=0, tiled=True),
        lax.all_to_all(send_energy, "grid", split_axis=0, concat_axis=0, tiled=True),
    )
    source_dev = supernode_of // width
    same_source = source_dev[:, None] == source_dev[None, :]
    before = supernode_of[None, :] < supernode_of[:, None]
    recv_rank = jnp.sum((same_source & before).astype(jnp.int32), axis=1)
    recv_slot = source_dev * slot_cap + recv_rank
    pickup = (recv_slot[:, None] == jnp.arange(grid_count * slot_cap)[None, :]).astype(jnp.bfloat16)
    density = jnp.dot(
        pickup,
        recv_dens.reshape(grid_count * slot_cap, row_width),
        preferred_element_type=jnp.float32,
    ).astype(jnp.bfloat16)
    energy = jnp.dot(
        pickup,
        recv_energy.reshape(grid_count * slot_cap, row_width),
        preferred_element_type=jnp.float32,
    ).astype(jnp.bfloat16)
    return (density, energy, electrons)


def solution(mesh):
    placed = (
        P("pole", "grid", None),
        P("pole", "grid", None, None, None),
        P("pole", "grid", None, None),
        P("grid", None, None),
        P("pole"),
        P("pole"),
        P("grid", None),
        P("grid"),
        P("grid", None),
        P("grid"),
        P("grid"),
    )
    return jax.shard_map(
        body,
        mesh=mesh,
        in_specs=placed,
        out_specs=(P("grid", "pole"), P("grid", "pole"), P()),
        check_vma=False,
    )
```

profile of v0, /device:TPU:0, one launch (start us, length us, event | category | flops | bytes accessed | tf_op | source)
XLA Modules:
  0.0 190.2 jit_solution(11743723445649057235)
XLA Ops:
  7.2 0.0 all-gather.3.cloned.1.call-start
  7.2 0.7 all-gather.3.cloned.1.call-update
  7.9 0.0 reduce-scatter.5.cloned.1.call-start
  9.9 0.7 convert_bitcast_fusion
  10.6 0.7 fusion.16
  11.3 1.0 broadcast_multiply_fusion
  12.3 79.9 %all-gather.3.cloned.1.call-done = bf16[1,1536,1536]{2,1,0:T(8,128)(2,1)} async-done(((bf16[1,192,1536]{2,1,0:T(8,128)(2,1)}), bf16[1,1536,1536]{2,1,0:T(8,128)(2,1)}) %all-gather.3.cloned.1.call-update) | async-done | bytes 4718608 | tf_op jit(solution)/shard_map/all_gather | solution.py:26
  92.2 6.7 %copy.25 = bf16[1,1536,1536]{1,2,0:T(8,128)(2,1)} copy(bf16[1,1536,1536]{2,1,0:T(8,128)(2,1)} %all-gather.3.cloned.1.call-done) | data formatting | bytes 9437184 | tf_op jit(solution)/shard_map/all_gather | solution.py:26
  99.0 8.7 %copy.26 = bf16[1536,6,256]{2,1,0:T(8,128)(2,1)} copy(bf16[1536,6,256]{0,2,1:T(8,128)(2,1)} %bitcast.50) | data formatting | bytes 9437184 | tf_op jit(solution)/shard_map/reshape | solution.py:30
  107.6 4.6 %fusion = bf16[1536,2,256]{2,1,0:T(2,128)(2,1)S(1)} fusion(bf16[1536,6,256]{2,1,0:T(8,128)(2,1)} %copy.26, s32[2]{0:T(128)S(1)} %bitcast.58), kind=kOutput, calls=%fused_computation.2 | convolution fusion | flops 10223628 | bytes 6291464 | tf_op jit(solution)/shard_map/rnw,mn->rmw/dot_general | solution.py:28
  112.3 1.1 reshape.95
  113.4 0.6 fusion.18
  113.9 0.3 multiply_reduce_fusion
  114.2 0.1 negate_multiply_fusion
  114.4 1.2 fusion.5
  115.5 1.3 fusion.2
  116.9 0.0 reduce-scatter.5.cloned.1.call-update
  116.9 0.0 reduce-scatter.3.cloned.1.call-start
  116.9 0.7 reduce-scatter.3.cloned.1.call-update
  117.6 0.2 convert_reduce_fusion
  117.8 0.2 convert_reduce_fusion.1
  118.7 38.6 %psum.7 = f32[]{:T(128)} all-reduce(f32[]{:T(128)S(6)} %mul.94), channel_id=1, replica_groups=mesh['pole'=4,'grid'=8] {'pole','grid'}, use_global_device_ids=true, to_apply=%region_6.7 | all-reduce | flops 1 | bytes 8 | tf_op jit(solution)/shard_map/psum | solution.py:49
  157.4 1.1 convolution_convert_fusion.2
  158.5 0.8 copy.29
  159.3 5.5 %all-to-all-start.1 = ((bf16[8,32,192]{2,1,0:T(8,128)(2,1)}), bf16[8,32,192]{2,1,0:T(8,128)(2,1)S(1)}, u32[]{:S(2)}, u32[]{:S(2)}) async-start(bf16[8,32,192]{2,1,0:T(8,128)(2,1)} %bitcast.20), calls=%async_computation.3 | async-start | bytes 262144 | tf_op jit(solution)/shard_map/all_to_all | solution.py:80
  164.8 1.1 convolution_convert_fusion.4
  165.9 0.8 copy.28
  166.7 5.4 %all-to-all-done.1 = bf16[8,32,192]{2,1,0:T(8,128)(2,1)S(1)} async-done(((bf16[8,32,192]{2,1,0:T(8,128)(2,1)}), bf16[8,32,192]{2,1,0:T(8,128)(2,1)S(1)}, u32[]{:S(2)}, u32[]{:S(2)}) %all-to-all-start.1) | async-done | bytes 98336 | tf_op jit(solution)/shard_map/all_to_all | solution.py:80
  172.1 3.4 %all-to-all-start = ((bf16[8,32,192]{2,1,0:T(8,128)(2,1)}), bf16[8,32,192]{2,1,0:T(8,128)(2,1)S(1)}, u32[]{:S(2)}, u32[]{:S(2)}) async-start(bf16[8,32,192]{2,1,0:T(8,128)(2,1)} %bitcast.15), calls=%async_computation.1 | async-start | bytes 262144 | tf_op jit(solution)/shard_map/all_to_all | solution.py:79
  175.5 0.9 convolution_convert_fusion.1
  176.4 6.3 %all-to-all-done = bf16[8,32,192]{2,1,0:T(8,128)(2,1)S(1)} async-done(((bf16[8,32,192]{2,1,0:T(8,128)(2,1)}), bf16[8,32,192]{2,1,0:T(8,128)(2,1)S(1)}, u32[]{:S(2)}, u32[]{:S(2)}) %all-to-all-start) | async-done | bytes 98336 | tf_op jit(solution)/shard_map/all_to_all | solution.py:79
  182.8 0.9 convolution_convert_fusion.3
  (19 shorter events, 0.1 us)
Async XLA Ops:
  7.2 85.1 %all-gather.3.cloned.1.call-start = ((), (), s32[]{:S(2)}) async-start(), calls=%async_computation.6 | async-start | bytes 5308416 | tf_op jit(solution)/shard_map/all_gather | solution.py:26
  7.9 149.5 %reduce-scatter.5.cloned.1.call-start = ((), (), s32[]{:S(2)}) async-start(), calls=%async_computation.5 | async-start | bytes 983040 | tf_op jit(solution)/shard_map/reduce_scatter | solution.py:54
  99.0 8.7 %copy-start.5 = (s32[1,2]{1,0:T(1,128)S(1)}, s32[1,2]{1,0:T(1,128)}, u32[]{:S(2)}) copy-start(s32[1,2]{1,0:T(1,128)} %param.17) | copy-start | bytes 28
  113.3 1.0 copy-start
  113.3 1.0 copy-start.1
  113.3 1.0 copy-start.2
  114.2 3.4 %copy-start.4 = (s32[256]{0:T(256)S(1)}, s32[256]{0:T(256)}, u32[]{:S(2)}) copy-start(s32[256]{0:T(256)} %param.20) | copy-start | bytes 3076
  114.2 3.6 %copy-start.3 = (s32[256]{0:T(256)S(1)}, s32[256]{0:T(256)}, u32[]{:S(2)}) copy-start(s32[256]{0:T(256)} %param.21) | copy-start | bytes 3076
  116.9 47.9 %reduce-scatter.3.cloned.1.call-start = ((), (), s32[]{:S(2)}) async-start(), calls=%async_computation.4 | async-start | bytes 983040 | tf_op jit(solution)/shard_map/reduce_scatter | solution.py:53
  159.3 12.8 %all-to-all-start.1 = ((bf16[8,32,192]{2,1,0:T(8,128)(2,1)}), bf16[8,32,192]{2,1,0:T(8,128)(2,1)S(1)}, u32[]{:S(2)}, u32[]{:S(2)}) async-start(bf16[8,32,192]{2,1,0:T(8,128)(2,1)} %bitcast.20), calls=%async_computation.3 | async-start | bytes 262144 | tf_op jit(solution)/shard_map/all_to_all | solution.py:80
  172.1 10.7 %all-to-all-start = ((bf16[8,32,192]{2,1,0:T(8,128)(2,1)}), bf16[8,32,192]{2,1,0:T(8,128)(2,1)S(1)}, u32[]{:S(2)}, u32[]{:S(2)}) async-start(bf16[8,32,192]{2,1,0:T(8,128)(2,1)} %bitcast.15), calls=%async_computation.1 | async-start | bytes 262144 | tf_op jit(solution)/shard_map/all_to_all | solution.py:79
Sparse Core Ops, SparseCore 0:
  10.2 82.0 all-gather.2
  117.0 21.6 reduce-scatter.4
  141.2 23.1 reduce-scatter.2
where the time goes:
time: 191 us; the launch traced here: 190 us
  waiting for transfers between devices  93.1 us (49%)
  blocking collectives  38.6 us (20%)
  local copies, waits for them, and re-layouts  18 us (9%)
  between operations  16.5 us (9%)
  matrix products  10.5 us (5%)
  starting transfers between devices  8.97 us (5%)
  other arithmetic  4.55 us (2%)
    all_gather x1, waiting for transfers between devices, body(): gathered = lax.all_gather(anc_inv[0], 'grid', axis=0, tiled=True)  79.9 us
    psum x1, blocking collectives, body(): electrons = lax.psum(own_count, ('pole', 'grid'))  38.6 us
    reshape x1, local copies, waits for them, and re-layouts, body(): gathered.reshape(row_count, anc_count, width)  8.66 us
    all_gather x1, local copies, waits for them, and re-layouts, body(): gathered = lax.all_gather(anc_inv[0], 'grid', axis=0, tiled=True)  6.72 us
    all_to_all x1, waiting for transfers between devices, body(): lax.all_to_all(send_dens, 'grid', split_axis=0, concat_axis=0, tiled=True)  6.35 us
    all_to_all x1, starting transfers between devices, body(): lax.all_to_all(send_energy, 'grid', split_axis=0, concat_axis=0, tiled=True)  5.48 us
    all_to_all x1, waiting for transfers between devices, body(): lax.all_to_all(send_energy, 'grid', split_axis=0, concat_axis=0, tiled=True)  5.42 us
    dot_general x1, matrix products, body(): jnp.einsum('rnw,mn->rmw', gathered.reshape(row_count, anc_count, width),...  4.62 us
  transfers between devices with their start and end apart: 5, of which 3 were waited for; matrix products, arithmetic and copies ran while one was open for 4% of the time, Pallas kernels for 0%

commit v1 on v0

--- a/solution.py
+++ b/solution.py
@@ -23,7 +23,23 @@
     select = (ancestors[0][:, None] == jnp.arange(anc_count)[None, :]).astype(jnp.bfloat16)
     live_mask = (jnp.arange(blk_count) < counts[0]).astype(jnp.bfloat16)
     lower_cols = (factor_cols[0, 0] * live_mask[:, None, None]).reshape(blk_count * width, width)
-    gathered = lax.all_gather(anc_inv[0], "grid", axis=0, tiled=True)
+
+    def keep_up_the_plane(x_part, group_axis):
+        current_arr = lax.axis_size(group_axis)
+        reached = lax.axis_index(group_axis)
+        finding, z2 = (current_arr, reached)
+        wide_out, s_next = (x_part, 1)
+        while s_next < finding:
+            arr_out = map(lambda m: (m, m ^ s_next), range(finding))
+            top = list(arr_out)
+            val = lax.ppermute(wide_out, axis_name=group_axis, perm=top)
+            item_now = jnp.concatenate([wide_out, val], axis=0)
+            y_new = jnp.concatenate([val, wide_out], axis=0)
+            wide_out = jnp.where(z2 & s_next == 0, item_now, y_new)
+            s_next = 2 * s_next
+        return wide_out
+
+    gathered = keep_up_the_plane(anc_inv[0], "grid")
     row_count = gathered.shape[0]
     picked = jnp.einsum(
         "rnw,mn->rmw",

time: 191 us -> 251 us (1.31)
  waiting for transfers between devices: 93.1 us -> 140 us
  starting transfers between devices: 8.97 us -> 17 us
  other arithmetic: 4.55 us -> 8.87 us
    ppermute x0 -> x3, waiting for transfers between devices: none -> 128 us  [keep_up_the_plane(): val = lax.ppermute(wide_out, axis_name=group_axis, perm=top)]
    all_gather x1 -> x0, waiting for transfers between devices: 79.9 us -> none  [body(): gathered = lax.all_gather(anc_inv[0], 'grid', axis=0, tiled=True)]
    concatenate x0 -> x4, local copies, waits for them, and re-layouts: none -> 9.7 us  [keep_up_the_plane(): item_now = jnp.concatenate([wide_out, val], axis=0)]
    reshape x1 -> x0, local copies, waits for them, and re-layouts: 8.66 us -> none  [body(): gathered.reshape(row_count, anc_count, width)]
    ppermute x0 -> x3, starting transfers between devices: none -> 7.45 us  [keep_up_the_plane(): val = lax.ppermute(wide_out, axis_name=group_axis, perm=top)]
    all_gather x1 -> x0, local copies, waits for them, and re-layouts: 6.72 us -> none  [body(): gathered = lax.all_gather(anc_inv[0], 'grid', axis=0, tiled=True)]
    select_n x0 -> x4, other arithmetic: none -> 5.87 us  [keep_up_the_plane(): wide_out = jnp.where(z2 & s_next == 0, item_now, y_new)]
  transfers between devices with their start and end apart: 5 -> 7, of which waited for: 3 -> 6; matrix products, arithmetic and copies ran while one was open for 4% -> 6% of each run, Pallas kernels for 0% -> 0%
where the time goes in v1:
time: 251 us
  waiting for transfers between devices  140 us (56%)
  blocking collectives  39.4 us (16%)
  starting transfers between devices  17 us (7%)
  local copies, waits for them, and re-layouts  16.8 us (7%)
  between operations  16.8 us (7%)
  matrix products  11.5 us (5%)
  other arithmetic  8.87 us (4%)
    ppermute x3, waiting for transfers between devices, keep_up_the_plane(): val = lax.ppermute(wide_out, axis_name=group_axis, perm=top)  128 us
    psum x1, blocking collectives, body(): electrons = lax.psum(own_count, ('pole', 'grid'))  39.4 us
    concatenate x4, local copies, waits for them, and re-layouts, keep_up_the_plane(): item_now = jnp.concatenate([wide_out, val], axis=0)  9.7 us
    ppermute x3, starting transfers between devices, keep_up_the_plane(): val = lax.ppermute(wide_out, axis_name=group_axis, perm=top)  7.45 us
    all_to_all x1, waiting for transfers between devices, body(): lax.all_to_all(send_dens, 'grid', split_axis=0, concat_axis=0, tiled=True)  6.35 us
    all_to_all x1, starting transfers between devices, body(): lax.all_to_all(send_energy, 'grid', split_axis=0, concat_axis=0, tiled=True)  6.12 us
    select_n x4, other arithmetic, keep_up_the_plane(): wide_out = jnp.where(z2 & s_next == 0, item_now, y_new)  5.87 us
    dot_general x1, matrix products, body(): jnp.einsum('rnw,mn->rmw', gathered.reshape(row_count, anc_count, width),...  5.64 us
  transfers between devices with their start and end apart: 7, of which 6 were waited for; matrix products, arithmetic and copies ran while one was open for 6% of the time, Pallas kernels for 0%

profile of v1, /device:TPU:0, one launch (start us, length us, event | category | flops | bytes accessed | tf_op | source)
XLA Modules:
  0.0 250.5 jit_solution(2468960225905282964)
XLA Ops:
  7.2 3.1 %collective-permute-start = (bf16[192,1536]{1,0:T(8,128)(2,1)}, bf16[192,1536]{1,0:T(8,128)(2,1)S(1)}, u32[]{:S(2)}, u32[]{:S(2)}) collective-permute-start(bf16[192,1536]{1,0:T(8,128)(2,1)} %bitcast.56), channel_id=1, source_target_pairs={{0,1},{1,0},{2,3},{3,2},{4,5},{5,4},{6,7},{7,6},{8,9},{9,8},{10,11... | collective-permute-start | bytes 1769480 | tf_op jit(solution)/shard_map/ppermute | solution.py:35
  10.3 1.4 copy.35
  11.6 12.2 %collective-permute-done = bf16[192,1536]{1,0:T(8,128)(2,1)S(1)} collective-permute-done((bf16[192,1536]{1,0:T(8,128)(2,1)}, bf16[192,1536]{1,0:T(8,128)(2,1)S(1)}, u32[]{:S(2)}, u32[]{:S(2)}) %collective-permute-start) | collective-permute-done | bytes 589856 | tf_op jit(solution)/shard_map/ppermute | solution.py:35
  24.6 0.9 maximum_select_fusion.9
  25.5 1.9 collective-permute-start.1
  27.4 25.3 %collective-permute-done.1 = bf16[384,1536]{0,1:T(8,128)(2,1)S(1)} collective-permute-done((bf16[384,1536]{0,1:T(8,128)(2,1)S(1)}, bf16[384,1536]{0,1:T(8,128)(2,1)S(1)}, u32[]{:S(2)}, u32[]{:S(2)}) %collective-permute-start.1) | collective-permute-done | bytes 1179680 | tf_op jit(solution)/shard_map/ppermute | solution.py:35
  52.7 1.8 maximum_select_fusion.3
  54.5 2.5 %collective-permute-start.2 = (bf16[768,1536]{0,1:T(8,128)(2,1)}, bf16[768,1536]{0,1:T(8,128)(2,1)}, u32[]{:S(2)}, u32[]{:S(2)}) collective-permute-start(bf16[768,1536]{0,1:T(8,128)(2,1)} %maximum_select_fusion.3), channel_id=1, source_target_pairs={{0,4},{1,5},{2,6},{3,7},{4,0},{5,1},{6,2},{7,3},{8,12},{9,13},{10,... | collective-permute-start | bytes 7077896 | tf_op jit(solution)/shard_map/ppermute | solution.py:35
  57.0 0.6 concatenate.43
  59.7 0.8 broadcast_multiply_fusion
  60.5 1.7 concatenate.44
  62.2 0.7 maximum_select_fusion.6
  62.9 2.3 copy.39
  65.2 2.6 %maximum_select_fusion.2 = bf16[768,6,256]{2,1,0:T(8,128)(2,1)} fusion(bf16[384,6,256]{2,1,0:T(8,128)(2,1)S(1)} %copy.39, bf16[384,6,256]{2,1,0:T(8,128)(2,1)S(1)} %maximum_select_fusion.6, pred[]{:T(512)S(6)} %eq.103), kind=kLoop, calls=%fused_computation.8 | loop fusion | flops 3538944 | bytes 4718593 | tf_op jit(solution)/shard_map/jit(_where)/select_n | solution.py:38
  67.7 90.1 %collective-permute-done.2 = bf16[768,1536]{0,1:T(8,128)(2,1)} collective-permute-done((bf16[768,1536]{0,1:T(8,128)(2,1)}, bf16[768,1536]{0,1:T(8,128)(2,1)}, u32[]{:S(2)}, u32[]{:S(2)}) %collective-permute-start.2) | collective-permute-done | bytes 2359328 | tf_op jit(solution)/shard_map/ppermute | solution.py:35
  157.8 5.1 %copy.41 = bf16[768,6,256]{2,1,0:T(8,128)(2,1)} copy(bf16[768,6,256]{0,2,1:T(8,128)(2,1)} %bitcast.9) | data formatting | bytes 4718592 | tf_op jit(solution)/shard_map/concatenate | solution.py:36
  162.9 5.6 %fusion.8 = bf16[1536,2,256]{2,1,0:T(2,128)(2,1)} fusion(bf16[768,6,256]{2,1,0:T(8,128)(2,1)} %copy.41, bf16[768,6,256]{2,1,0:T(8,128)(2,1)S(1)} %copy-done.1, pred[]{:T(512)S(6)} %eq.102, s32[2]{0:T(128)S(1)} %bitcast.62), kind=kOutput, calls=%fused_computation.13 | convolution fusion | flops 31457292 | bytes 6291465 | tf_op jit(solution)/shard_map/rnw,mn->rmw/dot_general | solution.py:44
  168.6 2.8 %reshape.106 = bf16[6,256,512]{2,1,0:T(8,128)(2,1)S(1)} reshape(bf16[1536,2,256]{2,1,0:T(2,128)(2,1)} %fusion.8) | data formatting | bytes 3145728 | tf_op jit(solution)/shard_map/reshape.46
  172.9 1.2 fusion.13
  174.1 1.3 fusion.10
  175.5 0.7 reduce-scatter.3.cloned.1.call-update
  177.3 39.4 %psum.7 = f32[]{:T(128)} all-reduce(f32[]{:T(128)S(6)} %mul.94), channel_id=1, replica_groups=mesh['pole'=4,'grid'=8] {'pole','grid'}, use_global_device_ids=true, to_apply=%region_6.7 | all-reduce | flops 1 | bytes 8 | tf_op jit(solution)/shard_map/psum | solution.py:65
  216.7 1.1 convolution_convert_fusion.1
  217.9 0.8 copy.45
  218.7 6.1 %all-to-all-start.1 = ((bf16[8,32,192]{2,1,0:T(8,128)(2,1)}), bf16[8,32,192]{2,1,0:T(8,128)(2,1)S(1)}, u32[]{:S(2)}, u32[]{:S(2)}) async-start(bf16[8,32,192]{2,1,0:T(8,128)(2,1)} %bitcast.23), calls=%async_computation.3 | async-start | bytes 262144 | tf_op jit(solution)/shard_map/all_to_all | solution.py:96
  225.4 1.1 convolution_convert_fusion.3
  226.5 0.8 copy.44
  227.3 4.8 %all-to-all-done.1 = bf16[8,32,192]{2,1,0:T(8,128)(2,1)S(1)} async-done(((bf16[8,32,192]{2,1,0:T(8,128)(2,1)}), bf16[8,32,192]{2,1,0:T(8,128)(2,1)S(1)}, u32[]{:S(2)}, u32[]{:S(2)}) %all-to-all-start.1) | async-done | bytes 98336 | tf_op jit(solution)/shard_map/all_to_all | solution.py:96
  232.1 3.4 %all-to-all-start = ((bf16[8,32,192]{2,1,0:T(8,128)(2,1)}), bf16[8,32,192]{2,1,0:T(8,128)(2,1)S(1)}, u32[]{:S(2)}, u32[]{:S(2)}) async-start(bf16[8,32,192]{2,1,0:T(8,128)(2,1)} %bitcast.18), calls=%async_computation.1 | async-start | bytes 262144 | tf_op jit(solution)/shard_map/all_to_all | solution.py:95
  235.5 0.9 convolution_convert_fusion
  236.4 6.3 %all-to-all-done = bf16[8,32,192]{2,1,0:T(8,128)(2,1)S(1)} async-done(((bf16[8,32,192]{2,1,0:T(8,128)(2,1)}), bf16[8,32,192]{2,1,0:T(8,128)(2,1)S(1)}, u32[]{:S(2)}, u32[]{:S(2)}) %all-to-all-start) | async-done | bytes 98336 | tf_op jit(solution)/shard_map/all_to_all | solution.py:95
  242.8 0.9 convolution_convert_fusion.2
  (42 shorter events, 3.6 us)
Async XLA Ops:
  7.2 209.6 %reduce-scatter.5.cloned.1.call-start = ((), (), s32[]{:S(2)}) async-start(), calls=%async_computation.5 | async-start | bytes 983040 | tf_op jit(solution)/shard_map/reduce_scatter | solution.py:70
  7.2 16.6 %collective-permute-start = (bf16[192,1536]{1,0:T(8,128)(2,1)}, bf16[192,1536]{1,0:T(8,128)(2,1)S(1)}, u32[]{:S(2)}, u32[]{:S(2)}) collective-permute-start(bf16[192,1536]{1,0:T(8,128)(2,1)} %bitcast.56), channel_id=1, source_target_pairs={{0,1},{1,0},{2,3},{3,2},{4,5},{5,4},{6,7},{7,6},{8,9},{9,8},{10,11... | collective-permute-start | bytes 1769480 | tf_op jit(solution)/shard_map/ppermute | solution.py:35
  23.8 0.8 copy-start.3
  25.5 27.2 %collective-permute-start.1 = (bf16[384,1536]{0,1:T(8,128)(2,1)S(1)}, bf16[384,1536]{0,1:T(8,128)(2,1)S(1)}, u32[]{:S(2)}, u32[]{:S(2)}) collective-permute-start(bf16[384,1536]{0,1:T(8,128)(2,1)S(1)} %maximum_select_fusion.9), channel_id=1, source_target_pairs={{0,2},{1,3},{2,0},{3,1},{4,6},{5,7},{6,4},{7,5},{8,10},{9,11},{10,... | collective-permute-start | bytes 3538952 | tf_op jit(solution)/shard_map/ppermute | solution.py:35
  27.4 29.6 %copy-start.2 = (bf16[1,192,1536]{2,1,0:T(8,128)(2,1)S(1)}, bf16[1,192,1536]{2,1,0:T(8,128)(2,1)}, u32[]{:S(2)}) copy-start(bf16[1,192,1536]{2,1,0:T(8,128)(2,1)} %param.11) | copy-start | bytes 1769476
  27.4 32.2 %copy-start.10 = (s32[1,2]{1,0:T(1,128)S(1)}, s32[1,2]{1,0:T(1,128)}, u32[]{:S(2)}) copy-start(s32[1,2]{1,0:T(1,128)} %param.19) | copy-start | bytes 28
  27.4 32.3 %copy-start.11 = (s32[1,2]{1,0:T(1,128)S(1)}, s32[1,2]{1,0:T(1,128)}, u32[]{:S(2)}) copy-start(s32[1,2]{1,0:T(1,128)} %param.17) | copy-start | bytes 28
  27.4 32.3 %copy-start.4 = (bf16[1,1,2,256,256]{4,3,2,1,0:T(8,128)(2,1)S(1)}, bf16[1,1,2,256,256]{4,3,2,1,0:T(8,128)(2,1)}, u32[]{:S(2)}) copy-start(bf16[1,1,2,256,256]{4,3,2,1,0:T(8,128)(2,1)} %param.12) | copy-start | bytes 786436
  52.7 1.8 copy-start
  54.5 103.3 %collective-permute-start.2 = (bf16[768,1536]{0,1:T(8,128)(2,1)}, bf16[768,1536]{0,1:T(8,128)(2,1)}, u32[]{:S(2)}, u32[]{:S(2)}) collective-permute-start(bf16[768,1536]{0,1:T(8,128)(2,1)} %maximum_select_fusion.3), channel_id=1, source_target_pairs={{0,4},{1,5},{2,6},{3,7},{4,0},{5,1},{6,2},{7,3},{8,12},{9,13},{10,... | collective-permute-start | bytes 7077896 | tf_op jit(solution)/shard_map/ppermute | solution.py:35
  157.8 5.1 %copy-start.1 = (bf16[768,6,256]{2,1,0:T(8,128)(2,1)S(1)}, bf16[768,6,256]{2,1,0:T(8,128)(2,1)}, u32[]{:S(2)}) copy-start(bf16[768,6,256]{2,1,0:T(8,128)(2,1)} %maximum_select_fusion.2) | copy-start | bytes 7077892
  168.6 2.8 %copy-start.5 = (bf16[1,1,2,256,256]{4,3,2,1,0:T(8,128)(2,1)S(1)}, bf16[1,1,2,256,256]{4,3,2,1,0:T(8,128)(2,1)}, u32[]{:S(2)}) copy-start(bf16[1,1,2,256,256]{4,3,2,1,0:T(8,128)(2,1)} %broadcast_multiply_fusion) | copy-start | bytes 786436
  172.0 0.9 copy-start.6
  172.0 1.0 copy-start.7
  172.9 3.3 %copy-start.9 = (s32[256]{0:T(256)S(1)}, s32[256]{0:T(256)}, u32[]{:S(2)}) copy-start(s32[256]{0:T(256)} %param.20) | copy-start | bytes 3076
  172.9 3.5 %copy-start.8 = (s32[256]{0:T(256)S(1)}, s32[256]{0:T(256)}, u32[]{:S(2)}) copy-start(s32[256]{0:T(256)} %param.21) | copy-start | bytes 3076
  175.4 50.0 %reduce-scatter.3.cloned.1.call-start = ((), (), s32[]{:S(2)}) async-start(), calls=%async_computation.4 | async-start | bytes 983040 | tf_op jit(solution)/shard_map/reduce_scatter | solution.py:69
  218.7 13.5 %all-to-all-start.1 = ((bf16[8,32,192]{2,1,0:T(8,128)(2,1)}), bf16[8,32,192]{2,1,0:T(8,128)(2,1)S(1)}, u32[]{:S(2)}, u32[]{:S(2)}) async-start(bf16[8,32,192]{2,1,0:T(8,128)(2,1)} %bitcast.23), calls=%async_computation.3 | async-start | bytes 262144 | tf_op jit(solution)/shard_map/all_to_all | solution.py:96
  232.1 10.7 %all-to-all-start = ((bf16[8,32,192]{2,1,0:T(8,128)(2,1)}), bf16[8,32,192]{2,1,0:T(8,128)(2,1)S(1)}, u32[]{:S(2)}, u32[]{:S(2)}) async-start(bf16[8,32,192]{2,1,0:T(8,128)(2,1)} %bitcast.18), calls=%async_computation.1 | async-start | bytes 262144 | tf_op jit(solution)/shard_map/all_to_all | solution.py:95
Sparse Core Ops, SparseCore 0:
  175.6 24.0 reduce-scatter.4
  202.1 23.2 reduce-scatter.2
